TPU v7x, 32 devices: a whole 2x2x4 slice. The times are simulated.
32 devices in a mesh: row: 4 (over z), col: 8 (over y, x, core).
Axes of the slice: x: 2, y: 2, z: 4, core: 2. Of those that a mesh axis runs over, the one named last changes fastest.
Arguments:
- weight: float32 [16384, 16384], P('row', 'col'), may hold values from -0.046875 to 0.046875
- leak: float32 [16384], P('col'), may hold values from 0.1 to 1
- rates: float32 [3, 256, 16384], P(None, 'row', 'col'), may hold values from -0.95 to 0.95
- cotangent: float32 [256, 16384], P('row', 'col'), may hold values from -2 to 2
Outputs:
- grad_input: float32 [256, 16384], P('row', 'col')
- grad_weight: float32 [16384, 16384], P('row', 'col')
- grad_noise: float32 [3, 16384], P(None, 'row')
All inputs are finite; a program needn't handle non-finite values.
Results may differ from a plain program's by a relative error of at most 0.0001.
Values sent between devices are 32-bit elements; how exact they have to be, the bound alone decides.
A program may use at most 192 MiB of HBM per device.

v0:
```python
import jax
import jax.numpy as jnp
from jax import lax
from jax.sharding import PartitionSpec as P

TSTEPS = 3


def shards(weight, leak, rates, cotangent):
    n_col = lax.axis_size("col")
    own_rows = cotangent.shape[0]
    local_units = cotangent.shape[1]
    full_rates = lax.all_gather(rates, "row", axis=1, tiled=True)
    grad_weight = jnp.zeros(weight.shape, jnp.float32)
    noise_list = []
    carried = cotangent
    for step_back in range(TSTEPS - 1, -1, -1):
        scaled = leak[None, :] * carried
        spread = scaled.reshape(own_rows, local_units // n_col, n_col)
        by_col = lax.all_to_all(spread, "col", split_axis=2, concat_axis=1, tiled=True)
        by_row = lax.all_to_all(by_col, "row", split_axis=1, concat_axis=0, tiled=True)
        gathered = lax.all_gather(by_row, "col", axis=2, tiled=True)
        unit_block = gathered.reshape(gathered.shape[0], gathered.shape[1] * gathered.shape[2])
        rates_now = full_rates[step_back]
        noise_list.insert(0, jnp.sum(unit_block, axis=0))
        grad_weight = grad_weight + lax.dot_general(
            unit_block,
            rates_now,
            (((0,), (0,)), ((), ())),
            precision=lax.Precision.HIGHEST,
            preferred_element_type=jnp.float32,
        )
        partial_sum = jnp.dot(
            unit_block, weight, precision=lax.Precision.HIGHEST, preferred_element_type=jnp.float32
        )
        adjoint = lax.psum_scatter(partial_sum, "row", scatter_dimension=0, tiled=True)
        local_rates = rates[step_back]
        carried = (1.0 - leak[None, :]) * carried + (1.0 - local_rates * local_rates) * adjoint
    return (carried, grad_weight, jnp.stack(noise_list))


def solution(mesh):
    placed = (P("row", "col"), P("col"), P(None, "row", "col"), P("row", "col"))
    return jax.shard_map(
        shards,
        mesh=mesh,
        in_specs=placed,
        out_specs=(P("row", "col"), P("row", "col"), P(None, "row")),
        check_vma=False,
    )
```

profile of v0, /device:TPU:0, one launch (start us, length us, event | category | flops | bytes accessed | tf_op | source)
XLA Modules:
  0.0 634.5 jit_solution(5892808969612367369)
XLA Ops:
  9.0 14.7 %all_to_all.108 = f32[64,256,8]{1,0,2:T(8,128)S(1)} all-to-all(f32[64,256,8]{1,0,2:T(8,128)S(1)} %copy.20), channel_id=1, replica_groups=mesh['row'=4,'col'=8] {'col'}, dimensions={2} | all-to-all | bytes 1048576 | tf_op jit(solution)/shard_map/all_to_all | solution.py:20
  24.6 9.3 %reduce.3 = f32[2048,64]{1,0:T(8,128)S(1)} reduce(f32[2048,1,64]{2,1,0:T(1,128)S(1)} %bitcast.75, f32[]{:T(128)} %broadcast.24), dimensions={1}, to_apply=%bitcast.64.reduce_sub_computation | reduce | bytes 1048580
  34.6 18.6 %all_to_all.109 = f32[4,1,32768]{2,1,0:T(1,128)S(1)} all-to-all(f32[4,1,32768]{2,1,0:T(1,128)S(1)} %reshape.48), channel_id=1, replica_groups=mesh['row'=4,'col'=8] {'row'}, dimensions={0} | all-to-all | bytes 1048576 | tf_op jit(solution)/shard_map/all_to_all | solution.py:21
  53.2 2.1 reduce.4
  58.3 34.2 %all-gather.5.cloned.1.call-done = f32[256,512,8]{1,0,2:T(8,128)} async-done(((f32[256,512,1]{1,0,2:T(8,128)}), f32[256,512,8]{1,0,2:T(8,128)}) %all-gather.5.cloned.1.call-update) | async-done | bytes 4194320 | tf_op jit(solution)/shard_map/all_gather | solution.py:22
  92.6 5.4 copy.25
  98.0 33.9 %fusion.9 = f32[256,2048]{1,0:T(8,128)} fusion(f32[4096,2048]{1,0:T(8,128)} %param.4, f32[256,512,8]{0,2,1:T(8,128)} %copy.25), kind=kOutput, calls=%fused_computation.10 | convolution fusion | flops 25769803776 | bytes 39845888 | tf_op jit(solution)/shard_map/dot_general | solution.py:33
  132.0 43.7 %reduce-scatter.4.cloned.1.call-done = f32[64,2048]{1,0:T(8,128)} async-done(((f32[256,2048]{1,0:T(8,128)}), f32[64,2048]{1,0:T(8,128)}) %reduce-scatter.4.cloned.1.call-update) | async-done | bytes 524304 | tf_op jit(solution)/shard_map/reduce_scatter | solution.py:36
  177.7 13.7 %all_to_all.110 = f32[64,256,8]{1,0,2:T(8,128)S(1)} all-to-all(f32[64,256,8]{1,0,2:T(8,128)S(1)} %copy.27), channel_id=1, replica_groups=mesh['row'=4,'col'=8] {'col'}, dimensions={2} | all-to-all | bytes 1048576 | tf_op jit(solution)/shard_map/all_to_all | solution.py:20
  191.8 9.3 %reduce.5 = f32[2048,64]{1,0:T(8,128)S(1)} reduce(f32[2048,1,64]{2,1,0:T(1,128)S(1)} %bitcast.76, f32[]{:T(128)} %broadcast.24), dimensions={1}, to_apply=%bitcast.66.reduce_sub_computation | reduce | bytes 1048580
  201.8 16.6 %all_to_all.111 = f32[4,1,32768]{2,1,0:T(1,128)S(1)} all-to-all(f32[4,1,32768]{2,1,0:T(1,128)S(1)} %reshape.50), channel_id=1, replica_groups=mesh['row'=4,'col'=8] {'row'}, dimensions={0} | all-to-all | bytes 1048576 | tf_op jit(solution)/shard_map/all_to_all | solution.py:21
  218.4 2.1 reduce.6
  223.4 34.3 %all-gather.7.cloned.1.call-done = f32[256,512,8]{1,0,2:T(8,128)} async-done(((f32[256,512,1]{1,0,2:T(8,128)}), f32[256,512,8]{1,0,2:T(8,128)}) %all-gather.7.cloned.1.call-update) | async-done | bytes 4194320 | tf_op jit(solution)/shard_map/all_gather | solution.py:22
  257.7 5.5 copy.32
  263.2 33.8 %fusion.5 = f32[256,2048]{1,0:T(8,128)} fusion(f32[4096,2048]{1,0:T(8,128)} %param.4, f32[256,512,8]{0,2,1:T(8,128)} %copy.32), kind=kOutput, calls=%fused_computation.6 | convolution fusion | flops 25769803776 | bytes 39845888 | tf_op jit(solution)/shard_map/dot_general | solution.py:33
  297.8 43.2 %reduce-scatter.6.cloned.1.call-done = f32[64,2048]{1,0:T(8,128)} async-done(((f32[256,2048]{1,0:T(8,128)}), f32[64,2048]{1,0:T(8,128)}) %reduce-scatter.6.cloned.1.call-update) | async-done | bytes 524304 | tf_op jit(solution)/shard_map/reduce_scatter | solution.py:36
  340.9 2.0 broadcast_multiply_fusion
  343.7 13.5 %all_to_all.112 = f32[64,256,8]{1,0,2:T(8,128)} all-to-all(f32[64,256,8]{1,0,2:T(8,128)S(1)} %copy.34), channel_id=1, replica_groups=mesh['row'=4,'col'=8] {'col'}, dimensions={2} | all-to-all | bytes 1048576 | tf_op jit(solution)/shard_map/all_to_all | solution.py:20
  358.5 10.3 %reduce.7 = f32[2048,64]{1,0:T(8,128)} reduce(f32[2048,1,64]{2,1,0:T(1,128)S(1)} %bitcast.77, f32[]{:T(128)} %broadcast.24), dimensions={1}, to_apply=%bitcast.68.reduce_sub_computation | reduce | bytes 1048580
  368.9 1.9 reshape.52
  370.7 32.0 %all_to_all.113 = f32[4,1,32768]{2,1,0:T(1,128)S(1)} all-to-all(f32[4,1,32768]{2,1,0:T(1,128)S(1)} %reshape.52), channel_id=1, replica_groups=mesh['row'=4,'col'=8] {'row'}, dimensions={0} | all-to-all | bytes 1048576 | tf_op jit(solution)/shard_map/all_to_all | solution.py:21
  402.7 2.1 reduce.8
  407.8 2.6 reduce_sum.29
  410.7 57.2 %all-gather.11.cloned.1.call-done = f32[3,256,2048]{2,1,0:T(8,128)} async-done(((f32[3,64,2048]{2,1,0:T(8,128)}), f32[3,256,2048]{2,1,0:T(8,128)}) %all-gather.11.cloned.1.call-update) | async-done | bytes 6291472 | tf_op jit(solution)/shard_map/all_gather | solution.py:13
  468.0 32.4 %fusion.7 = f32[4096,2048]{1,0:T(8,128)} fusion(f32[256,512,8]{0,2,1:T(8,128)} %copy.25, f32[3,256,2048]{2,1,0:T(8,128)} %all-gather.11.cloned.1.call-done), kind=kOutput, calls=%fused_computation.8 | convolution fusion | flops 25769803776 | bytes 39845888 | tf_op jit(solution)/shard_map/dot_general | solution.py:26
  500.4 2.7 reduce_sum.28
  503.4 32.7 %fusion.3 = f32[4096,2048]{1,0:T(8,128)} fusion(f32[256,512,8]{0,2,1:T(8,128)} %copy.32, f32[3,256,2048]{2,1,0:T(8,128)} %all-gather.11.cloned.1.call-done), kind=kOutput, calls=%fused_computation.4 | convolution fusion | flops 25769803776 | bytes 39845888 | tf_op jit(solution)/shard_map/dot_general | solution.py:26
  536.0 2.6 reduce_sum.27
  539.0 5.5 copy.39
  544.4 33.9 %fusion.1 = f32[256,2048]{1,0:T(8,128)} fusion(f32[4096,2048]{1,0:T(8,128)} %param.4, f32[256,512,8]{0,2,1:T(8,128)} %copy.39), kind=kOutput, calls=%fused_computation.2 | convolution fusion | flops 25769803776 | bytes 39845888 | tf_op jit(solution)/shard_map/dot_general | solution.py:33
  579.1 46.4 %add_add_fusion = f32[4096,2048]{1,0:T(8,128)} fusion(f32[4096,2048]{1,0:T(8,128)} %fusion.7, f32[4096,2048]{1,0:T(8,128)} %fusion.3, f32[256,512,8]{0,2,1:T(8,128)} %copy.39, f32[3,256,2048]{2,1,0:T(8,128)} %all-gather.11.cloned.1.call-done), kind=kOutput, calls=%fused_computation | convolution fusion | flops 25786580992 | bytes 106954752 | tf_op jit(solution)/shard_map/dot_general | solution.py:26
  625.4 1.9 fusion.11
  (57 shorter events, 19.4 us)
Async XLA Ops:
  7.2 85.4 %all-gather.5.cloned.1.call-start = ((), (), s32[]{:S(2)}) async-start(), calls=%async_computation.9 | async-start | bytes 4718592 | tf_op jit(solution)/shard_map/all_gather | solution.py:22
  58.0 117.7 %reduce-scatter.4.cloned.1.call-start = ((), (), s32[]{:S(2)}) async-start(), calls=%async_computation.10 | async-start | bytes 2621440 | tf_op jit(solution)/shard_map/reduce_scatter | solution.py:36
  98.0 33.9 %copy-start.4 = (f32[2048]{0:T(1024)S(1)}, f32[2048]{0:T(1024)}, u32[]{:S(2)}) copy-start(f32[2048]{0:T(1024)} %param.5) | copy-start | bytes 24580
  98.0 77.7 %copy-start.1 = (f32[64,2048]{1,0:T(8,128)S(1)}, f32[64,2048]{1,0:T(8,128)}, u32[]{:S(2)}) copy-start(f32[64,2048]{1,0:T(8,128)} %param.7) | copy-start | bytes 1572868
  131.9 125.9 %all-gather.7.cloned.1.call-start = ((), (), s32[]{:S(2)}) async-start(), calls=%async_computation.11 | async-start | bytes 4718592 | tf_op jit(solution)/shard_map/all_gather | solution.py:22
  223.2 117.7 %reduce-scatter.6.cloned.1.call-start = ((), (), s32[]{:S(2)}) async-start(), calls=%async_computation.12 | async-start | bytes 2621440 | tf_op jit(solution)/shard_map/reduce_scatter | solution.py:36
  263.2 77.7 %copy-start.3 = (f32[64,2048]{1,0:T(8,128)S(1)}, f32[64,2048]{1,0:T(8,128)}, u32[]{:S(2)}) copy-start(f32[64,2048]{1,0:T(8,128)} %reduce-scatter.4.cloned.1.call-done) | copy-start | bytes 1572868
  297.1 43.8 %copy-start = (f32[3,64,2048]{2,1,0:T(8,128)S(1)}, f32[3,64,2048]{2,1,0:T(8,128)}, u32[]{:S(2)}) copy-start(f32[3,64,2048]{2,1,0:T(8,128)} %param.6) | copy-start | bytes 4718596
  297.1 170.9 %all-gather.11.cloned.1.call-start = ((), (), s32[]{:S(2)}) async-start(), calls=%async_computation.15 | async-start | bytes 7864320 | tf_op jit(solution)/shard_map/all_gather | solution.py:13
  297.7 238.3 %all-gather.9.cloned.1.call-start = ((), (), s32[]{:S(2)}) async-start(), calls=%async_computation.13 | async-start | bytes 4718592 | tf_op jit(solution)/shard_map/all_gather | solution.py:22
  407.5 217.9 %reduce-scatter.8.cloned.1.call-start = ((), (), s32[]{:S(2)}) async-start(), calls=%async_computation.14 | async-start | bytes 2621440 | tf_op jit(solution)/shard_map/reduce_scatter | solution.py:36
  579.1 46.4 %copy-start.2 = (f32[64,2048]{1,0:T(8,128)S(1)}, f32[64,2048]{1,0:T(8,128)}, u32[]{:S(2)}) copy-start(f32[64,2048]{1,0:T(8,128)} %get-tuple-element.4) | copy-start | bytes 1572868
Sparse Core Ops, SparseCore 0:
  58.1 34.4 all-gather.4
  132.0 43.6 reduce-scatter.3
  223.3 34.4 all-gather.6
  297.2 43.6 reduce-scatter.5
  342.3 125.6 all-gather.10
  469.7 34.7 all-gather.8
  578.5 41.7 reduce-scatter.7
where the time goes:
time: 642 us; the launch traced here: 634 us
  waiting for transfers between devices  213 us (33%)
  matrix products  213 us (33%)
  blocking collectives  109 us (17%)
  other arithmetic  50.4 us (8%)
  local copies, waits for them, and re-layouts  33 us (5%)
  between operations  14.6 us (2%)
    dot_general x3, matrix products, shards(): lax.dot_general(unit_block, rates_now, (((0,), (0,)), ((), ())), precisio...  111 us
    dot_general x3, matrix products, shards(): jnp.dot(unit_block, weight, precision=lax.Precision.HIGHEST, preferred_el...  102 us
    reduce_scatter x3, waiting for transfers between devices, shards(): lax.psum_scatter(partial_sum, 'row', scatter_dimension=0, tiled=True)  86.9 us
    all_gather x3, waiting for transfers between devices, shards(): gathered = lax.all_gather(by_row, 'col', axis=2, tiled=True)  68.6 us
    all_to_all x3, blocking collectives, shards(): lax.all_to_all(by_col, 'row', split_axis=1, concat_axis=0, tiled=True)  67.2 us
    all_gather x1, waiting for transfers between devices, shards(): full_rates = lax.all_gather(rates, 'row', axis=1, tiled=True)  57.2 us
    all_to_all x3, blocking collectives, shards(): lax.all_to_all(spread, 'col', split_axis=2, concat_axis=1, tiled=True)  41.9 us
    unnamed x3, other arithmetic  29 us
  transfers between devices with their start and end apart: 7, of which 5 were waited for; matrix products, arithmetic and copies ran while one was open for 22% of the time, Pallas kernels for 0%

commit v1 on v0

--- a/solution.py
+++ b/solution.py
@@ -4,6 +4,20 @@
 from jax.sharding import PartitionSpec as P
 
 TSTEPS = 3
+
+
+def _process_row(local_x, ndim_at, q_in):
+    formed = local_x.shape
+    fresh = local_x.reshape(
+        *formed[:ndim_at], q_in, formed[ndim_at] // q_in, *formed[ndim_at + 1 :]
+    )
+    return jnp.moveaxis(fresh, ndim_at, 0)
+
+
+def draw_the_stages_all(vec, join_dim):
+    mat_out = list(vec.shape[1:])
+    mat_out[join_dim] *= vec.shape[0]
+    return jnp.moveaxis(vec, 0, join_dim).reshape(mat_out)
 
 
 def shards(weight, leak, rates, cotangent):
@@ -18,7 +32,22 @@
         scaled = leak[None, :] * carried
         spread = scaled.reshape(own_rows, local_units // n_col, n_col)
         by_col = lax.all_to_all(spread, "col", split_axis=2, concat_axis=1, tiled=True)
-        by_row = lax.all_to_all(by_col, "row", split_axis=1, concat_axis=0, tiled=True)
+
+        def use_the_table(row_data, content, arr_in, across):
+            lower = lax.axis_size(across)
+            z2 = lax.axis_index(across)
+            taken_in, n_now = (lower, z2)
+            response = _process_row(arr_in, row_data, taken_in)
+            parts_seen = [response[n_now]]
+            for q in range(1, taken_in):
+                block_last = response[n_now ^ q]
+                y2 = lax.ppermute(block_last, across, [(ix, ix ^ q) for ix in range(taken_in)])
+                parts_seen.append(y2)
+            carry_out = jnp.stack(parts_seen, axis=0)
+            response = carry_out[n_now ^ jnp.arange(taken_in)]
+            return draw_the_stages_all(response, content)
+
+        by_row = use_the_table(1, 0, arr_in=by_col, across="row")
         gathered = lax.all_gather(by_row, "col", axis=2, tiled=True)
         unit_block = gathered.reshape(gathered.shape[0], gathered.shape[1] * gathered.shape[2])
         rates_now = full_rates[step_back]

time: 642 us -> 613 us (0.955)
  blocking collectives: 109 us -> 26.5 us
  waiting for transfers between devices: 213 us -> 288 us
  other arithmetic: 50.4 us -> 15.1 us
  starting transfers between devices: 1 us -> 19.1 us
    all_to_all x3 -> x0, blocking collectives: 67.2 us -> none  [shards(): lax.all_to_all(by_col, 'row', split_axis=1, concat_axis=0, tiled=True)]
    ppermute x0 -> x9, waiting for transfers between devices: none -> 33 us  [use_the_table(): lax.ppermute(block_last, across, [(ix, ix ^ q) for ix in range(taken_in)])]
    unnamed x3 -> x0, other arithmetic: 29 us -> none
    all_gather x1, waiting for transfers between devices: 57.2 us -> 84.4 us  [shards(): full_rates = lax.all_gather(rates, 'row', axis=1, tiled=True)]
    all_to_all x3 -> x2, blocking collectives: 41.9 us -> 26.5 us  [shards(): lax.all_to_all(spread, 'col', split_axis=2, concat_axis=1, tiled=True)]
    ppermute x0 -> x9, starting transfers between devices: none -> 13.4 us  [use_the_table(): lax.ppermute(block_last, across, [(ix, ix ^ q) for ix in range(taken_in)])]
    all_to_all x0 -> x1, waiting for transfers between devices: none -> 9.65 us  [shards(): lax.all_to_all(spread, 'col', split_axis=2, concat_axis=1, tiled=True)]
    unnamed x17 -> x22, local copies, waits for them, and re-layouts: 7.58 us -> 0.14 us
  transfers between devices with their start and end apart: 7 -> 17, of which waited for: 5 -> 13; matrix products, arithmetic and copies ran while one was open for 22% -> 20% of each run, Pallas kernels for 0% -> 0%
where the time goes in v1:
time: 613 us; the launch traced here: 604 us
  waiting for transfers between devices  288 us (47%)
  matrix products  213 us (35%)
  local copies, waits for them, and re-layouts  27.5 us (4%)
  blocking collectives  26.5 us (4%)
  starting transfers between devices  19.1 us (3%)
  other arithmetic  15.1 us (2%)
  between operations  14.6 us (2%)
    dot_general x3, matrix products, shards(): lax.dot_general(unit_block, rates_now, (((0,), (0,)), ((), ())), precisio...  111 us
    dot_general x3, matrix products, shards(): jnp.dot(unit_block, weight, precision=lax.Precision.HIGHEST, preferred_el...  102 us
    reduce_scatter x3, waiting for transfers between devices, shards(): lax.psum_scatter(partial_sum, 'row', scatter_dimension=0, tiled=True)  86.9 us
    all_gather x1, waiting for transfers between devices, shards(): full_rates = lax.all_gather(rates, 'row', axis=1, tiled=True)  84.4 us
    all_gather x3, waiting for transfers between devices, shards(): gathered = lax.all_gather(by_row, 'col', axis=2, tiled=True)  73.9 us
    ppermute x9, waiting for transfers between devices, use_the_table(): lax.ppermute(block_last, across, [(ix, ix ^ q) for ix in range(taken_in)])  33 us
    all_to_all x2, blocking collectives, shards(): lax.all_to_all(spread, 'col', split_axis=2, concat_axis=1, tiled=True)  26.5 us
    all_gather x3, local copies, waits for them, and re-layouts, shards(): gathered = lax.all_gather(by_row, 'col', axis=2, tiled=True)  16.4 us
  transfers between devices with their start and end apart: 17, of which 13 were waited for; matrix products, arithmetic and copies ran while one was open for 20% of the time, Pallas kernels for 0%

profile of v1, /device:TPU:0, one launch (start us, length us, event | category | flops | bytes accessed | tf_op | source)
XLA Modules:
  0.0 604.4 jit_solution(4690669527978263931)
XLA Ops:
  9.8 5.2 all-to-all-start
  15.0 9.6 %all-to-all-done = f32[64,256,8]{1,0,2:T(8,128)S(1)} async-done(((f32[64,256,8]{1,0,2:T(8,128)}), f32[64,256,8]{1,0,2:T(8,128)S(1)}, u32[]{:S(2)}, u32[]{:S(2)}) %all-to-all-start) | async-done | bytes 524320 | tf_op jit(solution)/shard_map/all_to_all | solution.py:34
  25.8 1.6 collective-permute-start
  27.4 2.6 collective-permute-start.1
  31.3 6.7 %collective-permute-done.1 = f32[64,512,1]{1,0,2:T(8,128)S(1)} collective-permute-done((f32[64,512,1]{1,0,2:T(8,128)S(1)}, f32[64,512,1]{1,0,2:T(8,128)S(1)}, u32[]{:S(2)}, u32[]{:S(2)}) %collective-permute-start.1) | collective-permute-done | bytes 131104 | tf_op jit(solution)/shard_map/ppermute | solution.py:44
  39.5 38.0 %all-gather.5.cloned.1.call-done = f32[256,512,8]{1,0,2:T(8,128)} async-done(((f32[256,512,1]{1,0,2:T(8,128)}), f32[256,512,8]{1,0,2:T(8,128)}) %all-gather.5.cloned.1.call-update) | async-done | bytes 4194320 | tf_op jit(solution)/shard_map/all_gather | solution.py:51
  77.5 5.5 copy.31
  83.0 33.8 %fusion.9 = f32[256,2048]{1,0:T(8,128)} fusion(f32[4096,2048]{1,0:T(8,128)} %param.4, f32[256,512,8]{0,2,1:T(8,128)} %copy.31), kind=kOutput, calls=%fused_computation.13 | convolution fusion | flops 25769803776 | bytes 39845888 | tf_op jit(solution)/shard_map/dot_general | solution.py:62
  116.9 43.7 %reduce-scatter.4.cloned.1.call-done = f32[64,2048]{1,0:T(8,128)} async-done(((f32[256,2048]{1,0:T(8,128)}), f32[64,2048]{1,0:T(8,128)}) %reduce-scatter.4.cloned.1.call-update) | async-done | bytes 524304 | tf_op jit(solution)/shard_map/reduce_scatter | solution.py:65
  162.7 13.4 %all_to_all.45 = f32[64,256,8]{1,0,2:T(8,128)S(1)} all-to-all(f32[64,256,8]{1,0,2:T(8,128)S(1)} %copy.33), channel_id=1, replica_groups=mesh['row'=4,'col'=8] {'col'}, dimensions={2} | all-to-all | bytes 1048576 | tf_op jit(solution)/shard_map/all_to_all | solution.py:34
  179.3 2.3 collective-permute-start.5
  181.6 2.0 collective-permute-done.3
  183.6 6.6 %collective-permute-done.4 = f32[64,512,1]{1,0,2:T(8,128)S(1)} collective-permute-done((f32[64,512,1]{1,0,2:T(8,128)S(1)}, f32[64,512,1]{1,0,2:T(8,128)S(1)}, u32[]{:S(2)}, u32[]{:S(2)}) %collective-permute-start.4) | collective-permute-done | bytes 131104 | tf_op jit(solution)/shard_map/ppermute | solution.py:44
  191.7 36.0 %all-gather.7.cloned.1.call-done = f32[256,512,8]{1,0,2:T(8,128)} async-done(((f32[256,512,1]{1,0,2:T(8,128)}), f32[256,512,8]{1,0,2:T(8,128)}) %all-gather.7.cloned.1.call-update) | async-done | bytes 4194320 | tf_op jit(solution)/shard_map/all_gather | solution.py:51
  227.6 5.5 copy.35
  233.1 33.8 %fusion.5 = f32[256,2048]{1,0:T(8,128)} fusion(f32[4096,2048]{1,0:T(8,128)} %param.4, f32[256,512,8]{0,2,1:T(8,128)} %copy.35), kind=kOutput, calls=%fused_computation.9 | convolution fusion | flops 25769803776 | bytes 39845888 | tf_op jit(solution)/shard_map/dot_general | solution.py:62
  267.6 43.2 %reduce-scatter.6.cloned.1.call-done = f32[64,2048]{1,0:T(8,128)} async-done(((f32[256,2048]{1,0:T(8,128)}), f32[64,2048]{1,0:T(8,128)}) %reduce-scatter.6.cloned.1.call-update) | async-done | bytes 524304 | tf_op jit(solution)/shard_map/reduce_scatter | solution.py:65
  310.8 2.0 broadcast_multiply_fusion
  313.5 13.2 %all_to_all.46 = f32[64,256,8]{1,0,2:T(8,128)S(1)} all-to-all(f32[64,256,8]{1,0,2:T(8,128)S(1)} %copy.37), channel_id=1, replica_groups=mesh['row'=4,'col'=8] {'col'}, dimensions={2} | all-to-all | bytes 1048576 | tf_op jit(solution)/shard_map/all_to_all | solution.py:34
  330.0 2.3 collective-permute-start.8
  332.3 9.6 %collective-permute-done.6 = f32[64,512,1]{1,0,2:T(8,128)S(1)} collective-permute-done((f32[64,512,1]{1,0,2:T(8,128)S(1)}, f32[64,512,1]{1,0,2:T(8,128)S(1)}, u32[]{:S(2)}, u32[]{:S(2)}) %collective-permute-start.6) | collective-permute-done | bytes 131104 | tf_op jit(solution)/shard_map/ppermute | solution.py:44
  341.9 6.3 %collective-permute-done.7 = f32[64,512,1]{1,0,2:T(8,128)S(1)} collective-permute-done((f32[64,512,1]{1,0,2:T(8,128)S(1)}, f32[64,512,1]{1,0,2:T(8,128)S(1)}, u32[]{:S(2)}, u32[]{:S(2)}) %collective-permute-start.7) | collective-permute-done | bytes 131104 | tf_op jit(solution)/shard_map/ppermute | solution.py:44
  350.5 2.6 reduce_sum.29
  353.5 84.4 %all-gather.11.cloned.1.call-done = f32[3,256,2048]{2,1,0:T(8,128)} async-done(((f32[3,64,2048]{2,1,0:T(8,128)}), f32[3,256,2048]{2,1,0:T(8,128)}) %all-gather.11.cloned.1.call-update) | async-done | bytes 6291472 | tf_op jit(solution)/shard_map/all_gather | solution.py:27
  437.9 32.4 %fusion.7 = f32[4096,2048]{1,0:T(8,128)} fusion(f32[256,512,8]{0,2,1:T(8,128)} %copy.31, f32[3,256,2048]{2,1,0:T(8,128)} %all-gather.11.cloned.1.call-done), kind=kOutput, calls=%fused_computation.11 | convolution fusion | flops 25769803776 | bytes 39845888 | tf_op jit(solution)/shard_map/dot_general | solution.py:55
  470.2 2.7 reduce_sum.28
  473.2 32.5 %fusion.3 = f32[4096,2048]{1,0:T(8,128)} fusion(f32[256,512,8]{0,2,1:T(8,128)} %copy.35, f32[3,256,2048]{2,1,0:T(8,128)} %all-gather.11.cloned.1.call-done), kind=kOutput, calls=%fused_computation.7 | convolution fusion | flops 25769803776 | bytes 39845888 | tf_op jit(solution)/shard_map/dot_general | solution.py:55
  505.7 2.6 reduce_sum.27
  508.6 5.5 copy.39
  514.1 34.2 %fusion.1 = f32[256,2048]{1,0:T(8,128)} fusion(f32[4096,2048]{1,0:T(8,128)} %param.4, f32[256,512,8]{0,2,1:T(8,128)} %copy.39), kind=kOutput, calls=%fused_computation.5 | convolution fusion | flops 25769803776 | bytes 39845888 | tf_op jit(solution)/shard_map/dot_general | solution.py:62
  549.0 46.4 %add_add_fusion = f32[4096,2048]{1,0:T(8,128)} fusion(f32[4096,2048]{1,0:T(8,128)} %fusion.7, f32[4096,2048]{1,0:T(8,128)} %fusion.3, f32[256,512,8]{0,2,1:T(8,128)} %copy.39, f32[3,256,2048]{2,1,0:T(8,128)} %all-gather.11.cloned.1.call-done), kind=kOutput, calls=%fused_computation.3 | convolution fusion | flops 25786580992 | bytes 106954752 | tf_op jit(solution)/shard_map/dot_general | solution.py:55
  595.4 1.9 fusion.11
  (80 shorter events, 21.7 us)
Async XLA Ops:
  9.8 14.9 %all-to-all-start = ((f32[64,256,8]{1,0,2:T(8,128)}), f32[64,256,8]{1,0,2:T(8,128)S(1)}, u32[]{:S(2)}, u32[]{:S(2)}) async-start(f32[64,256,8]{1,0,2:T(8,128)} %copy.29), calls=%async_computation | async-start | bytes 1048576 | tf_op jit(solution)/shard_map/all_to_all | solution.py:34
  15.0 62.5 %all-gather.5.cloned.1.call-start = ((), (), s32[]{:S(2)}) async-start(), calls=%async_computation.6 | async-start | bytes 4718592 | tf_op jit(solution)/shard_map/all_gather | solution.py:51
  25.8 5.5 collective-permute-start
  27.4 10.6 %collective-permute-start.1 = (f32[64,512,1]{1,0,2:T(8,128)S(1)}, f32[64,512,1]{1,0,2:T(8,128)S(1)}, u32[]{:S(2)}, u32[]{:S(2)}) collective-permute-start(f32[64,512,1]{1,0,2:T(8,128)S(1)} %bitcast.140), channel_id=1, source_target_pairs={{0,16},{8,24},{16,0},{24,8},{1,17},{9,25},{17,1},{25,9},{2,18},{10... | collective-permute-start | bytes 393224 | tf_op jit(solution)/shard_map/ppermute | solution.py:44
  30.0 8.0 %collective-permute-start.2 = (f32[64,512,1]{1,0,2:T(8,128)S(1)}, f32[64,512,1]{1,0,2:T(8,128)S(1)}, u32[]{:S(2)}, u32[]{:S(2)}) collective-permute-start(f32[64,512,1]{1,0,2:T(8,128)S(1)} %bitcast.137), channel_id=1, source_target_pairs={{0,24},{8,16},{16,8},{24,0},{1,25},{9,17},{17,9},{25,1},{2,26},{10... | collective-permute-start | bytes 393224 | tf_op jit(solution)/shard_map/ppermute | solution.py:44
  39.5 121.2 %reduce-scatter.4.cloned.1.call-start = ((), (), s32[]{:S(2)}) async-start(), calls=%async_computation.7 | async-start | bytes 2621440 | tf_op jit(solution)/shard_map/reduce_scatter | solution.py:65
  83.0 33.9 %copy-start.4 = (f32[2048]{0:T(1024)S(1)}, f32[2048]{0:T(1024)}, u32[]{:S(2)}) copy-start(f32[2048]{0:T(1024)} %param.5) | copy-start | bytes 24580
  83.0 77.7 %copy-start.1 = (f32[64,2048]{1,0:T(8,128)S(1)}, f32[64,2048]{1,0:T(8,128)}, u32[]{:S(2)}) copy-start(f32[64,2048]{1,0:T(8,128)} %param.7) | copy-start | bytes 1572868
  116.9 110.8 %all-gather.7.cloned.1.call-start = ((), (), s32[]{:S(2)}) async-start(), calls=%async_computation.8 | async-start | bytes 4718592 | tf_op jit(solution)/shard_map/all_gather | solution.py:51
  177.1 6.4 %collective-permute-start.3 = (f32[64,512,1]{1,0,2:T(8,128)S(1)}, f32[64,512,1]{1,0,2:T(8,128)S(1)}, u32[]{:S(2)}, u32[]{:S(2)}) collective-permute-start(f32[64,512,1]{1,0,2:T(8,128)S(1)} %bitcast.144), channel_id=1, source_target_pairs={{0,8},{8,0},{16,24},{24,16},{1,9},{9,1},{17,25},{25,17},{2,10},{10... | collective-permute-start | bytes 393224 | tf_op jit(solution)/shard_map/ppermute | solution.py:44
  177.8 12.3 %collective-permute-start.4 = (f32[64,512,1]{1,0,2:T(8,128)S(1)}, f32[64,512,1]{1,0,2:T(8,128)S(1)}, u32[]{:S(2)}, u32[]{:S(2)}) collective-permute-start(f32[64,512,1]{1,0,2:T(8,128)S(1)} %bitcast.141), channel_id=1, source_target_pairs={{0,16},{8,24},{16,0},{24,8},{1,17},{9,25},{17,1},{25,9},{2,18},{10... | collective-permute-start | bytes 393224 | tf_op jit(solution)/shard_map/ppermute | solution.py:44
  179.3 10.9 %collective-permute-start.5 = (f32[64,512,1]{1,0,2:T(8,128)S(1)}, f32[64,512,1]{1,0,2:T(8,128)S(1)}, u32[]{:S(2)}, u32[]{:S(2)}) collective-permute-start(f32[64,512,1]{1,0,2:T(8,128)S(1)} %bitcast.138), channel_id=1, source_target_pairs={{0,24},{8,16},{16,8},{24,0},{1,25},{9,17},{17,9},{25,1},{2,26},{10... | collective-permute-start | bytes 393224 | tf_op jit(solution)/shard_map/ppermute | solution.py:44
  191.6 119.1 %reduce-scatter.6.cloned.1.call-start = ((), (), s32[]{:S(2)}) async-start(), calls=%async_computation.9 | async-start | bytes 2621440 | tf_op jit(solution)/shard_map/reduce_scatter | solution.py:65
  233.1 77.7 %copy-start.3 = (f32[64,2048]{1,0:T(8,128)S(1)}, f32[64,2048]{1,0:T(8,128)}, u32[]{:S(2)}) copy-start(f32[64,2048]{1,0:T(8,128)} %reduce-scatter.4.cloned.1.call-done) | copy-start | bytes 1572868
  267.0 43.8 %copy-start = (f32[3,64,2048]{2,1,0:T(8,128)S(1)}, f32[3,64,2048]{2,1,0:T(8,128)}, u32[]{:S(2)}) copy-start(f32[3,64,2048]{2,1,0:T(8,128)} %param.6) | copy-start | bytes 4718596
  267.0 170.9 %all-gather.11.cloned.1.call-start = ((), (), s32[]{:S(2)}) async-start(), calls=%async_computation.12 | async-start | bytes 7864320 | tf_op jit(solution)/shard_map/all_gather | solution.py:27
  267.6 238.1 %all-gather.9.cloned.1.call-start = ((), (), s32[]{:S(2)}) async-start(), calls=%async_computation.10 | async-start | bytes 4718592 | tf_op jit(solution)/shard_map/all_gather | solution.py:51
  327.8 14.1 %collective-permute-start.6 = (f32[64,512,1]{1,0,2:T(8,128)S(1)}, f32[64,512,1]{1,0,2:T(8,128)S(1)}, u32[]{:S(2)}, u32[]{:S(2)}) collective-permute-start(f32[64,512,1]{1,0,2:T(8,128)S(1)} %bitcast.145), channel_id=1, source_target_pairs={{0,8},{8,0},{16,24},{24,16},{1,9},{9,1},{17,25},{25,17},{2,10},{10... | collective-permute-start | bytes 393224 | tf_op jit(solution)/shard_map/ppermute | solution.py:44
  328.5 19.7 %collective-permute-start.7 = (f32[64,512,1]{1,0,2:T(8,128)S(1)}, f32[64,512,1]{1,0,2:T(8,128)S(1)}, u32[]{:S(2)}, u32[]{:S(2)}) collective-permute-start(f32[64,512,1]{1,0,2:T(8,128)S(1)} %bitcast.142), channel_id=1, source_target_pairs={{0,16},{8,24},{16,0},{24,8},{1,17},{9,25},{17,1},{25,9},{2,18},{10... | collective-permute-start | bytes 393224 | tf_op jit(solution)/shard_map/ppermute | solution.py:44
  330.0 18.9 %collective-permute-start.8 = (f32[64,512,1]{1,0,2:T(8,128)S(1)}, f32[64,512,1]{1,0,2:T(8,128)S(1)}, u32[]{:S(2)}, u32[]{:S(2)}) collective-permute-start(f32[64,512,1]{1,0,2:T(8,128)S(1)} %bitcast.139), channel_id=1, source_target_pairs={{0,24},{8,16},{16,8},{24,0},{1,25},{9,17},{17,9},{25,1},{2,26},{10... | collective-permute-start | bytes 393224 | tf_op jit(solution)/shard_map/ppermute | solution.py:44
  350.3 245.1 %reduce-scatter.8.cloned.1.call-start = ((), (), s32[]{:S(2)}) async-start(), calls=%async_computation.11 | async-start | bytes 2621440 | tf_op jit(solution)/shard_map/reduce_scatter | solution.py:65
  549.0 46.4 %copy-start.2 = (f32[64,2048]{1,0:T(8,128)S(1)}, f32[64,2048]{1,0:T(8,128)}, u32[]{:S(2)}) copy-start(f32[64,2048]{1,0:T(8,128)} %get-tuple-element.4) | copy-start | bytes 1572868
Sparse Core Ops, SparseCore 0:
  39.6 37.8 all-gather.4
  117.0 43.6 reduce-scatter.3
  191.7 35.8 all-gather.6
  267.1 43.6 reduce-scatter.5
  312.2 125.6 all-gather.10
  439.6 34.7 all-gather.8
  548.5 41.7 reduce-scatter.7
